TPU v7x, 32 devices: a whole 2x2x4 slice. The times are simulated.
32 devices in a mesh: seq: 8 (over y, x, core), tp: 4 (over z).
Axes of the slice: x: 2, y: 2, z: 4, core: 2. Of those that a mesh axis runs over, the one named last changes fastest.
Arguments:
- layer_input: bfloat16 [8192, 2048], P('seq', 'tp'), may hold values from -18 to 18
- gain_one: float32 [2048], P('tp'), may hold values from 0.25 to 1.75
- query_weight: bfloat16 [2048, 2048], P('seq', 'tp'), may hold values from -0.13258252 to 0.13258252
- key_weight: bfloat16 [2048, 2048], P('seq', 'tp'), may hold values from -0.13258252 to 0.13258252
- value_weight: bfloat16 [2048, 4096], P('seq', 'tp'), may hold values from -0.13258252 to 0.13258252
- gate_weight: bfloat16 [2048, 4096], P('seq', 'tp'), may hold values from -0.13258252 to 0.13258252
- out_weight: bfloat16 [4096, 2048], P('tp', 'seq'), may hold values from -0.13258252 to 0.13258252
- gain_two: float32 [2048], P('tp'), may hold values from 0.25 to 1.75
- up_weight: bfloat16 [2048, 4096], P(None, 'tp'), may hold values from -0.13258252 to 0.13258252
- down_weight: bfloat16 [4096, 2048], P('tp'), may hold values from -0.13258252 to 0.13258252
- cotangent: bfloat16 [8192, 2048], P('seq', 'tp'), may hold values from -6 to 6
Outputs:
- layer_output: bfloat16 [8192, 2048], P('seq', 'tp')
- input_grad: bfloat16 [8192, 2048], P('seq', 'tp')
- gain_one_grad: float32 [2048], P('tp')
- query_weight_grad: float32 [2048, 2048], P('seq', 'tp')
- key_weight_grad: float32 [2048, 2048], P('seq', 'tp')
- value_weight_grad: float32 [2048, 4096], P('seq', 'tp')
- gate_weight_grad: float32 [2048, 4096], P('seq', 'tp')
- out_weight_grad: float32 [4096, 2048], P('tp', 'seq')
- gain_two_grad: float32 [2048], P('tp')
- up_weight_grad: float32 [2048, 4096], P(None, 'tp')
- down_weight_grad: float32 [4096, 2048], P('tp')
All inputs are finite; a program needn't handle non-finite values.
Results may differ from a plain program's by a relative error of at most 0.022.
Values may be sent and summed in bfloat16 or wider, within the bound.
No kernel may reach another device: no remote copies, remote signals or barrier semaphores. Data moves between devices by JAX's collectives and lax.ppermute only.
A program may use at most 192 MiB of HBM per device.

v0:
```python
import math
import jax
import jax.numpy as jnp
from jax import lax
from jax.sharding import PartitionSpec as P

D = 2048
KEY_DIM = 256
VAL_DIM = 512
BLOCK = 512
MAXLEN = 8192
norm_eps = 1e-05
group_eps = 1.0
highest_precision_mode = lax.Precision.HIGHEST


def entering(array, axis, join, neutral, backward):
    count = lax.axis_size(axis)
    place = lax.axis_index(axis)
    ahead = count - 1 - place if backward else place
    gathered = jax.tree.map(
        lambda a, kind: lax.all_gather(a.astype(kind), axis), array, (jnp.bfloat16, jnp.bfloat16)
    )
    state = jax.tree.map(lambda a, e: jnp.zeros_like(a) + jnp.asarray(e, a.dtype), array, neutral)

    def one(lap, state):
        source = count - 1 - lap if backward else lap
        return join(
            state,
            jax.tree.map(
                lambda a, own: lax.dynamic_index_in_dim(a, source, 0, False).astype(own.dtype),
                gathered,
                array,
            ),
        )

    return lax.fori_loop(0, ahead, one, state)


def feature_gather(tensor):
    return lax.all_gather(tensor, "tp", axis=1, tiled=True)


def feature_sum(tensor):
    return lax.psum_scatter(
        tensor.astype(jnp.bfloat16), "tp", scatter_dimension=1, tiled=True
    ).astype(jnp.float32)


def row_totals(linear, squared):
    return lax.psum((linear, squared), "tp")


def norm_forward(tensor):
    linear, squared = row_totals(jnp.sum(tensor, axis=1), jnp.sum(tensor * tensor, axis=1))
    average = linear / D
    factor = lax.rsqrt(squared / D - average * average + norm_eps)
    return ((tensor - average[:, None]) * factor[:, None], factor)


def norm_backward(upstream, gain_part, normed, factor):
    shaped = upstream * gain_part
    linear, squared = row_totals(jnp.sum(shaped, axis=1), jnp.sum(shaped * normed, axis=1))
    result = factor[:, None] * (shaped - linear[:, None] / D - normed * squared[:, None] / D)
    return (result, jnp.sum(upstream * normed, axis=0))


def rotary_tables(positions, halfway):
    frequency = jnp.exp(-math.log(10000.0) * jnp.arange(halfway, dtype=jnp.float32) / halfway)
    angles = positions.astype(jnp.float32)[:, None] * frequency[None, :]
    return (jnp.cos(angles), jnp.sin(angles))


def rotate(tensor, cosine, sine_table):
    halfway = tensor.shape[-1] // 2
    former = tensor[..., :halfway]
    latter = tensor[..., halfway:]
    cos_part = cosine[:, None, :]
    sin_part = sine_table[:, None, :]
    return jnp.concatenate(
        [former * cos_part - latter * sin_part, former * sin_part + latter * cos_part], axis=-1
    )


def rotate_back(tensor, cosine, sine_table):
    halfway = tensor.shape[-1] // 2
    former = tensor[..., :halfway]
    latter = tensor[..., halfway:]
    cos_part = cosine[:, None, :]
    sin_part = sine_table[:, None, :]
    return jnp.concatenate(
        [former * cos_part + latter * sin_part, latter * cos_part - former * sin_part], axis=-1
    )


def decay_tables(log_gamma, block_len):
    offsets = jnp.arange(block_len, dtype=jnp.float32)
    lagged = offsets[:, None] - offsets[None, :]
    within = jnp.where(
        lagged[None] >= 0.0, jnp.exp(jnp.maximum(lagged, 0.0)[None] * log_gamma[:, None, None]), 0.0
    )
    outward_result = jnp.exp((offsets + 1.0)[None, :] * log_gamma[:, None])
    inward = jnp.exp((block_len - 1.0 - offsets)[None, :] * log_gamma[:, None])
    return (within, outward_result.T, inward.T)


def gate_mix(gate_raw, retained, head_count):
    grouped = retained.reshape(retained.shape[0], head_count, -1)
    centered = grouped - jnp.mean(grouped, axis=-1, keepdims=True)
    normed = centered * lax.rsqrt(jnp.mean(centered * centered, axis=-1, keepdims=True) + group_eps)
    return jax.nn.silu(gate_raw) * normed.reshape(gate_raw.shape)


def compose(earlier, later):
    return (earlier[0] * later[0], later[0][:, None, None] * earlier[1] + later[1])


def local(
    layer_input,
    gain_one,
    query_weight,
    key_weight,
    value_weight,
    gate_weight,
    out_weight,
    gain_two,
    up_weight,
    down_weight,
    cotangent,
):
    tok_rows = layer_input.shape[0]
    head_count = query_weight.shape[1] // KEY_DIM
    block_count = tok_rows // BLOCK
    seq_devices = lax.axis_size("seq")
    seq_length = min(MAXLEN, tok_rows * seq_devices)
    own_index = lax.axis_index("seq")
    first_pos = own_index * tok_rows % seq_length
    carries = jnp.where(first_pos == 0, 0.0, 1.0).astype(jnp.float32)
    head_ids = lax.axis_index("tp") * head_count + jnp.arange(head_count)
    log_gamma = jnp.log(1.0 - jnp.exp2(-5.0 - head_ids.astype(jnp.float32)))
    within, outward_result, inward = decay_tables(log_gamma, BLOCK)
    block_decay_factor = jnp.exp(BLOCK * log_gamma)[:, None, None]
    device_decay = jnp.exp(tok_rows * log_gamma)
    block_steps = jnp.arange(block_count, dtype=jnp.float32)
    lead_decay = jnp.exp(block_steps[:, None] * BLOCK * log_gamma[None, :])
    tail_decay = jnp.exp((block_count - 1.0 - block_steps)[:, None] * BLOCK * log_gamma[None, :])
    out_scale = outward_result[None, :, :, None]
    in_scale = inward[None, :, :, None]
    positions = first_pos + jnp.arange(tok_rows)
    cosine, sine_table = rotary_tables(positions, KEY_DIM // 2)
    key_scale = 1.0 / math.sqrt(KEY_DIM)
    state_zeros = jnp.zeros((head_count, KEY_DIM, VAL_DIM), jnp.float32)
    x_float = layer_input.astype(jnp.float32)
    normed_one, factor_one = norm_forward(x_float)
    shared_one = feature_gather((normed_one * gain_one).astype(jnp.bfloat16))
    full_weights = (
        lax.all_gather(query_weight, "seq", axis=0, tiled=True),
        lax.all_gather(key_weight, "seq", axis=0, tiled=True),
        lax.all_gather(value_weight, "seq", axis=0, tiled=True),
        lax.all_gather(gate_weight, "seq", axis=0, tiled=True),
        lax.all_gather(out_weight, "seq", axis=1, tiled=True),
    )
    query_full, key_full, value_full, gate_full, out_full = full_weights
    query_raw = jnp.dot(shared_one, query_full, preferred_element_type=jnp.float32).reshape(
        tok_rows, head_count, KEY_DIM
    )
    key_raw = jnp.dot(shared_one, key_full, preferred_element_type=jnp.float32).reshape(
        tok_rows, head_count, KEY_DIM
    )
    query_low = rotate(query_raw, cosine, sine_table).astype(jnp.bfloat16)
    key_low = (rotate(key_raw, cosine, sine_table) * key_scale).astype(jnp.bfloat16)
    value_low = jnp.dot(shared_one, value_full, preferred_element_type=jnp.float32).astype(
        jnp.bfloat16
    )
    gate_raw = jnp.dot(shared_one, gate_full, preferred_element_type=jnp.float32)
    query_blocks = query_low.reshape(block_count, BLOCK, head_count, KEY_DIM)
    key_blocks = key_low.reshape(block_count, BLOCK, head_count, KEY_DIM)
    value_blocks = value_low.reshape(block_count, BLOCK, head_count, VAL_DIM)
    query_wide = query_blocks.astype(jnp.float32)
    value_wide = value_blocks.astype(jnp.float32)
    key_value_outer = in_scale * key_blocks.astype(jnp.float32)
    local_terms = jnp.einsum(
        "cmhk,cmhv->chkv", key_value_outer, value_wide, precision=highest_precision_mode
    )

    def advance(running, term):
        return (block_decay_factor * running + term, running)

    local_end, local_starts = lax.scan(advance, state_zeros, local_terms)
    identity = (jnp.ones((head_count,), jnp.float32), state_zeros)
    reached = entering((carries * device_decay, local_end), "seq", compose, identity, False)
    state_in = carries * reached[1]
    block_states = lead_decay[:, :, None, None] * state_in[None] + local_starts
    scores = jnp.einsum(
        "cnhk,cmhk->chnm", query_blocks, key_blocks, preferred_element_type=jnp.float32
    )
    weights = (scores * within[None]).astype(jnp.bfloat16)
    inside = jnp.einsum(
        "chnm,cmhv->cnhv", weights, value_blocks, preferred_element_type=jnp.float32
    )
    carried_state_sum = out_scale * jnp.einsum(
        "cnhk,chkv->cnhv", query_wide, block_states, precision=highest_precision_mode
    )
    retained = (inside + carried_state_sum).reshape(tok_rows, head_count * VAL_DIM)
    mixed = gate_mix(gate_raw, retained, head_count).astype(jnp.bfloat16)
    hidden = x_float + feature_sum(jnp.dot(mixed, out_full, preferred_element_type=jnp.float32))
    normed_two, factor_two = norm_forward(hidden)
    shared_local = (normed_two * gain_two).astype(jnp.bfloat16)
    cot_float = cotangent.astype(jnp.float32)
    shared_two = feature_gather(shared_local)
    cot_whole = feature_gather(cotangent)
    up_use, down_use = (up_weight, down_weight)
    up_pre = jnp.dot(shared_two, up_use, preferred_element_type=jnp.float32)
    activated = jax.nn.gelu(up_pre).astype(jnp.bfloat16)
    ffn_part = jnp.dot(activated, down_use, preferred_element_type=jnp.float32)
    ffn_out = feature_sum(ffn_part)
    result = hidden + ffn_out
    layer_output = result.astype(jnp.bfloat16)
    grad_act = jnp.einsum("rd,fd->rf", cot_whole, down_use, preferred_element_type=jnp.float32)
    down_grad = jnp.einsum("rf,rd->fd", activated, cot_whole, preferred_element_type=jnp.float32)
    _, gelu_pull = jax.vjp(jax.nn.gelu, up_pre)
    grad_up = gelu_pull(grad_act)[0].astype(jnp.bfloat16)
    up_grad = jnp.einsum("rd,rf->df", shared_two, grad_up, preferred_element_type=jnp.float32)
    grad_two_part = jnp.einsum("rf,df->rd", grad_up, up_use, preferred_element_type=jnp.float32)
    grad_two = feature_sum(grad_two_part)
    norm_two_back, gain_two_grad = norm_backward(grad_two, gain_two, normed_two, factor_two)
    grad_hidden = cot_float + norm_two_back
    grad_branch = feature_gather(grad_hidden.astype(jnp.bfloat16))
    query_back, key_back, value_back, gate_back, out_back = full_weights
    grad_mixed = jnp.einsum("rd,vd->rv", grad_branch, out_back, preferred_element_type=jnp.float32)
    out_grad = jnp.einsum("rv,rd->vd", mixed, grad_branch, preferred_element_type=jnp.float32)

    def gate_local(gate_input, retained_input):
        return gate_mix(gate_input, retained_input, head_count)

    _, mix_pull = jax.vjp(gate_local, gate_raw, retained)
    grad_gate_f, grad_retained_f = mix_pull(grad_mixed)
    grad_gate = grad_gate_f.astype(jnp.bfloat16)
    grad_out_blocks = grad_retained_f.astype(jnp.bfloat16).reshape(
        block_count, BLOCK, head_count, VAL_DIM
    )
    grad_out_wide = grad_out_blocks.astype(jnp.float32)
    scores_again = jnp.einsum(
        "cnhk,cmhk->chnm", query_blocks, key_blocks, preferred_element_type=jnp.float32
    )
    weights_again = (scores_again * within[None]).astype(jnp.bfloat16)
    grad_weights = jnp.einsum(
        "cnhv,cmhv->chnm", grad_out_blocks, value_blocks, preferred_element_type=jnp.float32
    )
    grad_scores = (grad_weights * within[None]).astype(jnp.bfloat16)
    grad_value = jnp.einsum(
        "chnm,cnhv->cmhv", weights_again, grad_out_blocks, preferred_element_type=jnp.float32
    )
    grad_query = jnp.einsum(
        "chnm,cmhk->cnhk", grad_scores, key_blocks, preferred_element_type=jnp.float32
    )
    grad_query = grad_query + out_scale * jnp.einsum(
        "cnhv,chkv->cnhk", grad_out_wide, block_states, precision=highest_precision_mode
    )
    grad_key = jnp.einsum(
        "chnm,cnhk->cmhk", grad_scores, query_blocks, preferred_element_type=jnp.float32
    )
    state_terms = jnp.einsum(
        "cnhk,cnhv->chkv", query_wide, out_scale * grad_out_wide, precision=highest_precision_mode
    )

    def retreat(running, term):
        updated = term + block_decay_factor * running
        return (updated, updated)

    _, local_grads = lax.scan(retreat, state_zeros, state_terms, reverse=True)
    local_first = local_grads[0]
    reached_back = entering(
        (carries * device_decay, carries * local_first), "seq", compose, identity, True
    )
    grad_end = reached_back[1]
    following = jnp.concatenate([local_grads[1:], jnp.zeros_like(local_grads[:1])], axis=0)
    grad_terms = following + tail_decay[:, :, None, None] * grad_end[None]
    grad_key = grad_key + in_scale * jnp.einsum(
        "cmhv,chkv->cmhk", value_wide, grad_terms, precision=highest_precision_mode
    )
    grad_value = grad_value + jnp.einsum(
        "cmhk,chkv->cmhv", key_value_outer, grad_terms, precision=highest_precision_mode
    )
    grad_query_raw = (
        rotate_back(grad_query.reshape(tok_rows, head_count, KEY_DIM), cosine, sine_table)
        .reshape(tok_rows, head_count * KEY_DIM)
        .astype(jnp.bfloat16)
    )
    grad_key_raw = (
        (
            rotate_back(grad_key.reshape(tok_rows, head_count, KEY_DIM), cosine, sine_table)
            * key_scale
        )
        .reshape(tok_rows, head_count * KEY_DIM)
        .astype(jnp.bfloat16)
    )
    grad_value_raw = grad_value.reshape(tok_rows, head_count * VAL_DIM).astype(jnp.bfloat16)
    query_grad = jnp.einsum(
        "rd,rk->dk", shared_one, grad_query_raw, preferred_element_type=jnp.float32
    )
    key_grad = jnp.einsum("rd,rk->dk", shared_one, grad_key_raw, preferred_element_type=jnp.float32)
    value_grad = jnp.einsum(
        "rd,rv->dv", shared_one, grad_value_raw, preferred_element_type=jnp.float32
    )
    gate_grad = jnp.einsum("rd,rv->dv", shared_one, grad_gate, preferred_element_type=jnp.float32)
    grad_shared = jnp.einsum(
        "rk,dk->rd", grad_query_raw, query_back, preferred_element_type=jnp.float32
    )
    grad_shared = grad_shared + jnp.einsum(
        "rk,dk->rd", grad_key_raw, key_back, preferred_element_type=jnp.float32
    )
    grad_shared = grad_shared + jnp.einsum(
        "rv,dv->rd", grad_value_raw, value_back, preferred_element_type=jnp.float32
    )
    grad_shared = grad_shared + jnp.einsum(
        "rv,dv->rd", grad_gate, gate_back, preferred_element_type=jnp.float32
    )
    grad_one = feature_sum(grad_shared)
    norm_one_back, gain_one_grad = norm_backward(grad_one, gain_one, normed_one, factor_one)
    input_grad = (grad_hidden + norm_one_back).astype(jnp.bfloat16)
    mixer_sums = (
        lax.psum_scatter(
            query_grad.astype(jnp.bfloat16), "seq", scatter_dimension=0, tiled=True
        ).astype(jnp.float32),
        lax.psum_scatter(
            key_grad.astype(jnp.bfloat16), "seq", scatter_dimension=0, tiled=True
        ).astype(jnp.float32),
        lax.psum_scatter(
            value_grad.astype(jnp.bfloat16), "seq", scatter_dimension=0, tiled=True
        ).astype(jnp.float32),
        lax.psum_scatter(
            gate_grad.astype(jnp.bfloat16), "seq", scatter_dimension=0, tiled=True
        ).astype(jnp.float32),
        lax.psum_scatter(
            out_grad.astype(jnp.bfloat16), "seq", scatter_dimension=1, tiled=True
        ).astype(jnp.float32),
    )
    ffn_sums = (
        lax.psum(up_grad.astype(jnp.bfloat16), "seq").astype(jnp.float32),
        lax.psum(down_grad.astype(jnp.bfloat16), "seq").astype(jnp.float32),
        lax.psum(gain_one_grad.astype(jnp.bfloat16), "seq").astype(jnp.float32),
        lax.psum(gain_two_grad.astype(jnp.bfloat16), "seq").astype(jnp.float32),
    )
    return (
        layer_output,
        input_grad,
        ffn_sums[2],
        mixer_sums[0],
        mixer_sums[1],
        mixer_sums[2],
        mixer_sums[3],
        mixer_sums[4],
        ffn_sums[3],
        ffn_sums[0],
        ffn_sums[1],
    )


def solution(mesh):
    placed = (
        P("seq", "tp"),
        P("tp"),
        P("seq", "tp"),
        P("seq", "tp"),
        P("seq", "tp"),
        P("seq", "tp"),
        P("tp", "seq"),
        P("tp"),
        P(None, "tp"),
        P("tp", None),
        P("seq", "tp"),
    )
    return jax.shard_map(
        local,
        mesh=mesh,
        in_specs=placed,
        out_specs=(
            P("seq", "tp"),
            P("seq", "tp"),
            P("tp"),
            P("seq", "tp"),
            P("seq", "tp"),
            P("seq", "tp"),
            P("seq", "tp"),
            P("tp", "seq"),
            P("tp"),
            P(None, "tp"),
            P("tp", None),
        ),
        check_vma=False,
    )
```

profile of v0, /device:TPU:0, one launch (start us, length us, event | category | flops | bytes accessed | tf_op | source)
XLA Modules:
  0.0 1420.9 jit_solution(11341853395114596802)
XLA Ops:
  9.6 13.7 all-reduce.4
  29.5 11.0 all-gather.22.cloned.1.call-done
  40.4 82.9 %all-gather.14.cloned.1.call-done = bf16[1024,2048]{1,0:T(8,128)(2,1)} async-done(((bf16[1024,512]{1,0:T(8,128)(2,1)}), bf16[1024,2048]{1,0:T(8,128)(2,1)}) %all-gather.14.cloned.1.call-update) | async-done | bytes 4194320 | tf_op jit(solution)/shard_map/all_gather | solution.py:41
  123.3 5.2 fusion.84
  133.7 17.9 %all-gather.20.cloned.1.call-done = bf16[2048,512]{1,0:T(8,128)(2,1)} async-done(((bf16[256,512]{1,0:T(8,128)(2,1)}), bf16[2048,512]{1,0:T(8,128)(2,1)}) %all-gather.20.cloned.1.call-update) | async-done | bytes 2097168 | tf_op jit(solution)/shard_map/all_gather | solution.py:157
  151.5 5.2 fusion.83
  166.6 23.2 %all-gather.18.cloned.1.call-done = bf16[2048,1024]{1,0:T(8,128)(2,1)} async-done(((bf16[256,1024]{1,0:T(8,128)(2,1)}), bf16[2048,1024]{1,0:T(8,128)(2,1)}) %all-gather.18.cloned.1.call-update) | async-done | bytes 4194320 | tf_op jit(solution)/shard_map/all_gather | solution.py:159
  189.9 9.3 convolution_convert_fusion.10
  202.6 4.8 fusion.50
  209.0 4.6 while.58
  215.9 8.7 all-gather.1
  232.0 19.3 %all-gather.34.cloned.1.call-done = bf16[16,256,512]{2,1,0:T(8,128)(2,1)} async-done(((bf16[2,256,512]{2,1,0:T(8,128)(2,1)}), bf16[16,256,512]{2,1,0:T(8,128)(2,1)}) %all-gather.34.cloned.1.call-update) | async-done | bytes 4194320 | tf_op jit(solution)/shard_map/all_gather | solution.py:22
  253.3 7.1 fusion.82
  260.5 7.6 copy.152
  274.5 15.1 %all-gather.16.cloned.1.call-done = bf16[2048,1024]{1,0:T(8,128)(2,1)} async-done(((bf16[256,1024]{1,0:T(8,128)(2,1)}), bf16[2048,1024]{1,0:T(8,128)(2,1)}) %all-gather.16.cloned.1.call-update) | async-done | bytes 4194320 | tf_op jit(solution)/shard_map/all_gather | solution.py:160
  289.6 12.8 multiply_convert_fusion.2
  302.4 26.5 %all-gather.24.cloned.1.call-done = bf16[1024,2048]{1,0:T(8,128)(2,1)} async-done(((bf16[1024,256]{1,0:T(8,128)(2,1)}), bf16[1024,2048]{1,0:T(8,128)(2,1)}) %all-gather.24.cloned.1.call-update) | async-done | bytes 4194320 | tf_op jit(solution)/shard_map/all_gather | solution.py:161
  328.8 9.4 convolution_convert_fusion.7
  339.5 75.8 %reduce-scatter.10.cloned.1.call-done = bf16[1024,512]{1,0:T(8,128)(2,1)} async-done(((bf16[1024,2048]{1,0:T(8,128)(2,1)}), bf16[1024,512]{1,0:T(8,128)(2,1)}) %reduce-scatter.10.cloned.1.call-update) | async-done | bytes 1048592 | tf_op jit(solution)/shard_map/reduce_scatter | solution.py:45
  417.0 11.1 all-reduce.3
  430.9 67.2 %all-gather.28.cloned.1.call-done = bf16[1024,2048]{1,0:T(8,128)(2,1)} async-done(((bf16[1024,512]{1,0:T(8,128)(2,1)}), bf16[1024,2048]{1,0:T(8,128)(2,1)}) %all-gather.28.cloned.1.call-update) | async-done | bytes 4194320 | tf_op jit(solution)/shard_map/all_gather | solution.py:41
  498.1 10.1 fusion.85
  508.1 71.2 %all-gather.26.cloned.1.call-done = bf16[1024,2048]{1,0:T(8,128)(2,1)} async-done(((bf16[1024,512]{1,0:T(8,128)(2,1)}), bf16[1024,2048]{1,0:T(8,128)(2,1)}) %all-gather.26.cloned.1.call-update) | async-done | bytes 4194320 | tf_op jit(solution)/shard_map/all_gather | solution.py:41
  579.3 13.9 fusion.10
  594.5 6.3 convolution_convert_fusion.5
  600.9 75.4 %reduce-scatter.14.cloned.1.call-done = bf16[1024,512]{1,0:T(8,128)(2,1)} async-done(((bf16[1024,2048]{1,0:T(8,128)(2,1)}), bf16[1024,512]{1,0:T(8,128)(2,1)}) %reduce-scatter.14.cloned.1.call-update) | async-done | bytes 1048592 | tf_op jit(solution)/shard_map/reduce_scatter | solution.py:45
  680.1 11.1 all-reduce.2
  695.2 4.6 copy.163
  699.8 74.6 %all-gather.30.cloned.1.call-done = bf16[1024,2048]{1,0:T(8,128)(2,1)} async-done(((bf16[1024,512]{1,0:T(8,128)(2,1)}), bf16[1024,2048]{1,0:T(8,128)(2,1)}) %all-gather.30.cloned.1.call-update) | async-done | bytes 4194320 | tf_op jit(solution)/shard_map/all_gather | solution.py:41
  774.4 14.5 %fusion.72 = (f32[1024,1024]{0,1:T(8,128)}, bf16[1024,1024]{0,1:T(8,128)(2,1)}) fusion(f32[1024,1024]{0,1:T(8,128)} %get-tuple-element.456, f32[1024,2]{0,1:T(2,128)S(1)} %rsqrt.18, f32[1024,1024]{0,1:T(8,128)} %bitcast.171, f32[1024,2]{0,1:T(2,128)S(1)} %bitcast.198, bf16[1024,2048]{1,0:T(8,128)(2,1)} %all-gather.30.cloned.1.call-done, ...), kind=kOutput, calls=%fused_computation.147 | convolution fusion | flops 4310695936 | bytes 23085056 | tf_op jit(solution)/shard_map/rd,vd->rv/dot_general | solution.py:230
  789.0 5.6 copy.164
  794.6 4.4 multiply_reduce_fusion
  806.5 4.5 reshape.451
  810.9 6.1 copy.167
  817.1 5.9 fusion.18
  824.6 5.3 while.59
  832.9 9.5 convolution_convert_fusion.1
  842.4 6.8 convolution_convert_fusion
  849.3 9.4 convolution_convert_fusion.2
  858.8 9.5 convolution_convert_fusion.3
  869.6 4.3 fusion.52
  881.8 9.9 while.57
  901.1 6.4 convolution_convert_fusion.9
  911.7 6.0 convolution_convert_fusion.8
  922.4 7.5 fusion.54
  936.7 6.3 convolution_convert_fusion.4
  944.6 6.5 fusion.89
  951.2 5.8 fusion.86
  957.0 6.8 fusion.88
  963.8 11.7 add_convert_fusion
  975.7 10.8 convolution_convert_fusion.6
  986.6 11.3 all-reduce.9.cloned.1.call-done
  997.9 6.8 convert_element_type.309
  1004.7 4.7 convert_element_type.311
  1009.4 42.9 %reduce-scatter.26.cloned.1.call-done = bf16[1024,256]{1,0:T(8,128)(2,1)} async-done(((bf16[1024,2048]{1,0:T(8,128)(2,1)}), bf16[1024,256]{1,0:T(8,128)(2,1)}) %reduce-scatter.26.cloned.1.call-update) | async-done | bytes 524304 | tf_op jit(solution)/shard_map/reduce_scatter | solution.py:335
  1054.4 52.3 %reduce-scatter.24.cloned.1.call-done = bf16[256,1024]{1,0:T(8,128)(2,1)} async-done(((bf16[2048,1024]{1,0:T(8,128)(2,1)}), bf16[256,1024]{1,0:T(8,128)(2,1)}) %reduce-scatter.24.cloned.1.call-update) | async-done | bytes 524304 | tf_op jit(solution)/shard_map/reduce_scatter | solution.py:332
  1108.8 42.1 %reduce-scatter.18.cloned.1.call-done = bf16[256,512]{1,0:T(8,128)(2,1)} async-done(((bf16[2048,512]{1,0:T(8,128)(2,1)}), bf16[256,512]{1,0:T(8,128)(2,1)}) %reduce-scatter.18.cloned.1.call-update) | async-done | bytes 262160 | tf_op jit(solution)/shard_map/reduce_scatter | solution.py:323
  1152.8 42.4 %reduce-scatter.20.cloned.1.call-done = bf16[256,512]{1,0:T(8,128)(2,1)} async-done(((bf16[2048,512]{1,0:T(8,128)(2,1)}), bf16[256,512]{1,0:T(8,128)(2,1)}) %reduce-scatter.20.cloned.1.call-update) | async-done | bytes 262160 | tf_op jit(solution)/shard_map/reduce_scatter | solution.py:326
  1197.0 52.7 %reduce-scatter.22.cloned.1.call-done = bf16[256,1024]{1,0:T(8,128)(2,1)} async-done(((bf16[2048,1024]{1,0:T(8,128)(2,1)}), bf16[256,1024]{1,0:T(8,128)(2,1)}) %reduce-scatter.22.cloned.1.call-update) | async-done | bytes 524304 | tf_op jit(solution)/shard_map/reduce_scatter | solution.py:329
  1251.8 76.8 %reduce-scatter.16.cloned.1.call-done = bf16[1024,512]{1,0:T(8,128)(2,1)} async-done(((bf16[1024,2048]{1,0:T(8,128)(2,1)}), bf16[1024,512]{1,0:T(8,128)(2,1)}) %reduce-scatter.16.cloned.1.call-update) | async-done | bytes 1048592 | tf_op jit(solution)/shard_map/reduce_scatter | solution.py:45
  1331.3 13.4 all-reduce.5
  1345.8 12.3 all-reduce.1
  1358.1 50.7 %reduce-scatter.12.cloned.1.call-done = bf16[1024,512]{1,0:T(8,128)(2,1)} async-done(((bf16[1024,2048]{1,0:T(8,128)(2,1)}), bf16[1024,512]{1,0:T(8,128)(2,1)}) %reduce-scatter.12.cloned.1.call-update) | async-done | bytes 1048592 | tf_op jit(solution)/shard_map/reduce_scatter | solution.py:45
  1408.9 5.0 fusion.36
  (279 shorter events, 142.5 us)
Async XLA Ops:
  7.2 33.2 %all-gather.22.cloned.1.call-start = ((), (), s32[]{:S(2)}) async-start(), calls=%async_computation.13 | async-start | bytes 2359296 | tf_op jit(solution)/shard_map/all_gather | solution.py:158
  7.9 115.4 %all-gather.14.cloned.1.call-start = ((), (), s32[]{:S(2)}) async-start(), calls=%async_computation.9 | async-start | bytes 5242880 | tf_op jit(solution)/shard_map/all_gather | solution.py:41
  23.3 4.1 copy-start.49
  23.3 4.1 copy-start.51
  26.0 125.5 %all-gather.20.cloned.1.call-start = ((), (), s32[]{:S(2)}) async-start(), calls=%async_computation.12 | async-start | bytes 2359296 | tf_op jit(solution)/shard_map/all_gather | solution.py:157
  26.7 163.2 %all-gather.18.cloned.1.call-start = ((), (), s32[]{:S(2)}) async-start(), calls=%async_computation.11 | async-start | bytes 4718592 | tf_op jit(solution)/shard_map/all_gather | solution.py:159
  27.3 223.9 %all-gather.34.cloned.1.call-start = ((), (), s32[]{:S(2)}) async-start(), calls=%async_computation.28 | async-start | bytes 4718592 | tf_op jit(solution)/shard_map/all_gather | solution.py:22
  27.5 175.1 %copy-start.43 = (f32[512,2]{0,1:T(2,128)}, f32[512,2]{0,1:T(2,128)S(1)}, u32[]{:S(2)}) copy-start(f32[512,2]{0,1:T(2,128)S(1)} %get-tuple-element.451) | copy-start | bytes 12292
  29.4 132.4 %copy-start.29 = (f32[1024,128]{1,0:T(8,128)}, f32[1024,128]{1,0:T(8,128)S(1)}, u32[]{:S(2)}) copy-start(f32[1024,128]{1,0:T(8,128)S(1)} %get-tuple-element.443) | copy-start | bytes 1572868
  29.4 132.4 %copy-start.31 = (f32[1024,128]{1,0:T(8,128)}, f32[1024,128]{1,0:T(8,128)S(1)}, u32[]{:S(2)}) copy-start(f32[1024,128]{1,0:T(8,128)S(1)} %get-tuple-element.444) | copy-start | bytes 1572868
  214.5 75.1 %all-gather.16.cloned.1.call-start = ((), (), s32[]{:S(2)}) async-start(), calls=%async_computation.10 | async-start | bytes 4718592 | tf_op jit(solution)/shard_map/all_gather | solution.py:160
  215.1 113.8 %all-gather.24.cloned.1.call-start = ((), (), s32[]{:S(2)}) async-start(), calls=%async_computation.14 | async-start | bytes 4718592 | tf_op jit(solution)/shard_map/all_gather | solution.py:161
  215.8 199.4 %reduce-scatter.10.cloned.1.call-start = ((), (), s32[]{:S(2)}) async-start(), calls=%async_computation.15 | async-start | bytes 5242880 | tf_op jit(solution)/shard_map/reduce_scatter | solution.py:45
  251.5 9.0 copy-start.10
  338.3 77.0 %copy-start.1 = (bf16[1024,512]{1,0:T(8,128)(2,1)S(1)}, bf16[1024,512]{1,0:T(8,128)(2,1)}, u32[]{:S(2)}) copy-start(bf16[1024,512]{1,0:T(8,128)(2,1)} %param.19) | copy-start | bytes 3145732
  338.3 89.8 %copy-start.55 = (f32[512]{0:T(512)S(1)}, f32[512]{0:T(512)}, u32[]{:S(2)}) copy-start(f32[512]{0:T(512)} %param.26) | copy-start | bytes 6148
  338.3 159.8 %all-gather.28.cloned.1.call-start = ((), (), s32[]{:S(2)}) async-start(), calls=%async_computation.18 | async-start | bytes 5242880 | tf_op jit(solution)/shard_map/all_gather | solution.py:41
  339.0 240.3 %all-gather.26.cloned.1.call-start = ((), (), s32[]{:S(2)}) async-start(), calls=%async_computation.16 | async-start | bytes 5242880 | tf_op jit(solution)/shard_map/all_gather | solution.py:41
  428.1 263.1 %copy-start.45 = (f32[1024]{0:T(1024)}, f32[1024]{0:T(1024)S(1)}, u32[]{:S(2)}) copy-start(f32[1024]{0:T(1024)S(1)} %get-tuple-element.445) | copy-start | bytes 12292
  428.1 263.1 %copy-start.47 = (f32[1024]{0:T(1024)}, f32[1024]{0:T(1024)S(1)}, u32[]{:S(2)}) copy-start(f32[1024]{0:T(1024)S(1)} %get-tuple-element.446) | copy-start | bytes 12292
  430.8 245.5 %reduce-scatter.14.cloned.1.call-start = ((), (), s32[]{:S(2)}) async-start(), calls=%async_computation.19 | async-start | bytes 5242880 | tf_op jit(solution)/shard_map/reduce_scatter | solution.py:45
  579.3 15.2 %copy-start.61 = (bf16[2048,1024]{1,0:T(8,128)(2,1)S(1)}, bf16[2048,1024]{1,0:T(8,128)(2,1)}, u32[]{:S(2)}) copy-start(bf16[2048,1024]{1,0:T(8,128)(2,1)} %param.27) | copy-start | bytes 12582916
  600.9 173.6 %all-gather.30.cloned.1.call-start = ((), (), s32[]{:S(2)}) async-start(), calls=%async_computation.20 | async-start | bytes 5242880 | tf_op jit(solution)/shard_map/all_gather | solution.py:41
  691.2 4.0 copy-start.58
  695.2 186.5 %all-gather.32.cloned.1.call-start = ((), (), s32[]{:S(2)}) async-start(), calls=%async_computation.21 | async-start | bytes 4718592 | tf_op jit(solution)/shard_map/all_gather | solution.py:22
  794.6 4.6 copy-start.6
  794.6 5.9 copy-start.7
  800.5 3.5 copy-start.5
  832.8 165.0 %all-reduce.9.cloned.1.call-start = ((), (), s32[]{:S(2)}) async-start(), calls=%async_computation.29 | async-start | bytes 16777216 | tf_op jit(solution)/shard_map/psum | solution.py:340
  832.9 9.6 copy-start.63
  832.9 9.6 copy-start.65
  849.3 203.0 %reduce-scatter.26.cloned.1.call-start = ((), (), s32[]{:S(2)}) async-start(), calls=%async_computation.27 | async-start | bytes 4718592 | tf_op jit(solution)/shard_map/reduce_scatter | solution.py:335
  858.8 247.9 %reduce-scatter.24.cloned.1.call-start = ((), (), s32[]{:S(2)}) async-start(), calls=%async_computation.26 | async-start | bytes 4718592 | tf_op jit(solution)/shard_map/reduce_scatter | solution.py:332
  868.4 282.5 %reduce-scatter.18.cloned.1.call-start = ((), (), s32[]{:S(2)}) async-start(), calls=%async_computation.23 | async-start | bytes 2359296 | tf_op jit(solution)/shard_map/reduce_scatter | solution.py:323
  869.6 4.3 copy-start.4
  869.6 4.3 copy-start.8
  891.7 3.6 copy-start.19
  891.7 3.6 copy-start.25
  891.8 3.6 copy-start.27
  891.8 3.6 copy-start.44
  901.1 6.4 copy-start.41
  907.5 287.6 %reduce-scatter.20.cloned.1.call-start = ((), (), s32[]{:S(2)}) async-start(), calls=%async_computation.24 | async-start | bytes 2359296 | tf_op jit(solution)/shard_map/reduce_scatter | solution.py:326
  917.7 332.0 %reduce-scatter.22.cloned.1.call-start = ((), (), s32[]{:S(2)}) async-start(), calls=%async_computation.25 | async-start | bytes 4718592 | tf_op jit(solution)/shard_map/reduce_scatter | solution.py:329
  936.2 6.8 copy-start.39
  943.0 385.7 %reduce-scatter.16.cloned.1.call-start = ((), (), s32[]{:S(2)}) async-start(), calls=%async_computation.22 | async-start | bytes 5242880 | tf_op jit(solution)/shard_map/reduce_scatter | solution.py:45
  944.6 6.5 copy-start.42
  944.6 6.6 copy-start.64
  951.2 5.8 copy-start.40
  951.2 5.8 copy-start.62
  957.0 6.8 copy-start.35
  975.5 433.3 %reduce-scatter.12.cloned.1.call-start = ((), (), s32[]{:S(2)}) async-start(), calls=%async_computation.17 | async-start | bytes 5242880 | tf_op jit(solution)/shard_map/reduce_scatter | solution.py:45
  997.9 6.8 copy-start.33
  1054.4 274.3 %copy-start.2 = (bf16[1024,512]{1,0:T(8,128)(2,1)S(1)}, bf16[1024,512]{1,0:T(8,128)(2,1)}, u32[]{:S(2)}) copy-start(bf16[1024,512]{1,0:T(8,128)(2,1)} %param.19) | copy-start | bytes 3145732
  1054.4 274.3 %copy-start.50 = (f32[1024]{0:T(1024)S(1)}, f32[1024]{0:T(1024)}, u32[]{:S(2)}) copy-start(f32[1024]{0:T(1024)} %copy-done.49) | copy-start | bytes 12292
  1054.4 274.3 %copy-start.52 = (f32[1024]{0:T(1024)S(1)}, f32[1024]{0:T(1024)}, u32[]{:S(2)}) copy-start(f32[1024]{0:T(1024)} %copy-done.51) | copy-start | bytes 12292
  1054.4 274.3 %copy-start.57 = (f32[512]{0:T(512)S(1)}, f32[512]{0:T(512)}, u32[]{:S(2)}) copy-start(f32[512]{0:T(512)} %param.20) | copy-start | bytes 6148
  1152.7 178.6 %copy-start.60 = (bf16[512]{0:T(512)(128)(2,1)S(1)}, bf16[512]{0:T(512)(128)(2,1)}, u32[]{:S(2)}) copy-start(bf16[512]{0:T(512)(128)(2,1)} %get-tuple-element.357) | copy-start | bytes 3076
  1152.7 256.1 %copy-start.15 = (bf16[1024,512]{1,0:T(8,128)(2,1)S(1)}, bf16[1024,512]{1,0:T(8,128)(2,1)}, u32[]{:S(2)}) copy-start(bf16[1024,512]{1,0:T(8,128)(2,1)} %reduce-scatter.10.cloned.1.call-done) | copy-start | bytes 3145732
  1152.7 256.1 %copy-start.22 = (bf16[1024,512]{1,0:T(8,128)(2,1)S(1)}, bf16[1024,512]{1,0:T(8,128)(2,1)}, u32[]{:S(2)}) copy-start(bf16[1024,512]{1,0:T(8,128)(2,1)} %reduce-scatter.14.cloned.1.call-done) | copy-start | bytes 3145732
  1152.7 256.1 %copy-start.46 = (f32[1024]{0:T(1024)S(1)}, f32[1024]{0:T(1024)}, u32[]{:S(2)}) copy-start(f32[1024]{0:T(1024)} %copy-done.45) | copy-start | bytes 12292
  1152.7 256.1 %copy-start.48 = (f32[1024]{0:T(1024)S(1)}, f32[1024]{0:T(1024)}, u32[]{:S(2)}) copy-start(f32[1024]{0:T(1024)} %copy-done.47) | copy-start | bytes 12292
  1152.7 256.1 %copy-start.54 = (f32[1024]{0:T(1024)S(1)}, f32[1024]{0:T(1024)}, u32[]{:S(2)}) copy-start(f32[1024]{0:T(1024)} %copy-done.53) | copy-start | bytes 12292
  1152.8 256.1 %copy-start.56 = (f32[512]{0:T(512)S(1)}, f32[512]{0:T(512)}, u32[]{:S(2)}) copy-start(f32[512]{0:T(512)} %param.26) | copy-start | bytes 6148
  1152.8 256.1 %copy-start.59 = (f32[1024]{0:T(1024)S(1)}, f32[1024]{0:T(1024)}, u32[]{:S(2)}) copy-start(f32[1024]{0:T(1024)} %copy-done.58) | copy-start | bytes 12292
  (25 other events, 46.1 us)
Sparse Core Ops, SparseCore 0:
  9.9 30.5 all-gather.21
  42.6 80.7 all-gather.13
  125.2 26.2 all-gather.19
  153.3 36.5 all-gather.17
  214.6 36.5 all-gather.33
  253.0 36.5 all-gather.15
  291.5 37.3 all-gather.23
  338.4 76.7 reduce-scatter.9
  416.8 81.2 all-gather.27
  500.1 79.2 all-gather.25
  601.0 75.2 reduce-scatter.13
  695.3 79.0 all-gather.29
  832.9 35.0 all-gather.31
  871.6 126.2 all-reduce.8
  1001.1 51.1 reduce-scatter.25
  1055.5 51.1 reduce-scatter.23
  1109.8 41.0 reduce-scatter.17
  1154.1 41.0 reduce-scatter.19
  1198.5 51.1 reduce-scatter.21
  1251.9 76.7 reduce-scatter.15
  1331.0 77.7 reduce-scatter.11
where the time goes:
time: 1430 us; the launch traced here: 1420 us
  waiting for transfers between devices  935 us (65%)
  matrix products  227 us (16%)
  other arithmetic  90.3 us (6%)
  local copies, waits for them, and re-layouts  79.9 us (6%)
  blocking collectives  70.4 us (5%)
  between operations  15.5 us (1%)
    all_gather x4, waiting for transfers between devices, feature_gather(): return lax.all_gather(tensor, 'tp', axis=1, tiled=True)  296 us
    reduce_scatter x4, waiting for transfers between devices, feature_sum(): lax.psum_scatter(tensor.astype(jnp.bfloat16), 'tp', scatter_dimension=1,...  279 us
    reduce_scatter x1, waiting for transfers between devices, local(): lax.psum_scatter(value_grad.astype(jnp.bfloat16), 'seq', scatter_dimensio...  52.7 us
    reduce_scatter x1, waiting for transfers between devices, local(): lax.psum_scatter(gate_grad.astype(jnp.bfloat16), 'seq', scatter_dimension...  52.3 us
    psum x4, blocking collectives, row_totals(): return lax.psum((linear, squared), 'tp')  48.3 us
    reduce_scatter x1, waiting for transfers between devices, local(): lax.psum_scatter(out_grad.astype(jnp.bfloat16), 'seq', scatter_dimension=...  42.9 us
    reduce_scatter x1, waiting for transfers between devices, local(): lax.psum_scatter(key_grad.astype(jnp.bfloat16), 'seq', scatter_dimension=...  42.4 us
    reduce_scatter x1, waiting for transfers between devices, local(): lax.psum_scatter(query_grad.astype(jnp.bfloat16), 'seq', scatter_dimensio...  42.1 us
  transfers between devices with their start and end apart: 21, of which 20 were waited for; matrix products, arithmetic and copies ran while one was open for 18% of the time, Pallas kernels for 0%

commit v1 on v0

--- a/solution.py
+++ b/solution.py
@@ -12,6 +12,24 @@
 norm_eps = 1e-05
 group_eps = 1.0
 highest_precision_mode = lax.Precision.HIGHEST
+
+
+def cube_note(base_x, array_axis):
+    x_now = list(base_x.shape[1:])
+    x_now[array_axis] *= base_x.shape[0]
+    return jnp.moveaxis(base_x, 0, array_axis).reshape(x_now)
+
+
+def show_the_chunk(raw, lane_axis):
+    a_now = raw[None]
+    n_shards = lax.psum(1, lane_axis)
+    for p in range(n_shards.bit_length() - 1):
+        answer = 1 << p
+        r1 = lax.ppermute(a_now, lane_axis, tuple(((s, s ^ answer) for s in range(n_shards))))
+        wide_out = jnp.stack([a_now, r1], 0)
+        after = lax.axis_index(lane_axis) >> p & 1
+        a_now = jnp.where(after == 0, wide_out, wide_out[::-1]).reshape(-1, *raw.shape)
+    return a_now
 
 
 def entering(array, axis, join, neutral, backward):
@@ -38,7 +56,11 @@
 
 
 def feature_gather(tensor):
-    return lax.all_gather(tensor, "tp", axis=1, tiled=True)
+
+    def run_check(where_dim, z, vec):
+        return cube_note(show_the_chunk(vec, z), where_dim)
+
+    return run_check(1, "tp", tensor)
 
 
 def feature_sum(tensor):

time: 1430 us -> 1550 us (1.084)
  starting transfers between devices: 2.22 us -> 45.8 us
  local copies, waits for them, and re-layouts: 79.9 us -> 116 us
  other arithmetic: 90.3 us -> 113 us
    ppermute x0 -> x8, waiting for transfers between devices: none -> 372 us  [show_the_chunk(): lax.ppermute(a_now, lane_axis, tuple(((s, s ^ answer) for s in range(n_sh...]
    all_gather x4 -> x0, waiting for transfers between devices: 296 us -> none  [feature_gather(): return lax.all_gather(tensor, 'tp', axis=1, tiled=True)]
    ppermute x0 -> x8, starting transfers between devices: none -> 44.8 us  [show_the_chunk(): lax.ppermute(a_now, lane_axis, tuple(((s, s ^ answer) for s in range(n_sh...]
    reshape x0 -> x5, local copies, waits for them, and re-layouts: none -> 31.7 us  [the longest x3 18.8 us: show_the_chunk(): jnp.where(after == 0, wide_out, wide_out[::-1]).reshape(-1, *raw.shape)]
    all_gather x1, waiting for transfers between devices: 23.2 us -> 0.02 us  [local(): lax.all_gather(value_weight, 'seq', axis=0, tiled=True)]
    another operation x1 -> x16, other arithmetic: 3.68 us -> 25.8 us  [the longest x15 24.3 us: show_the_chunk(): wide_out = jnp.stack([a_now, r1], 0)]
    reduce_scatter x4, waiting for transfers between devices: 279 us -> 260 us  [feature_sum(): lax.psum_scatter(tensor.astype(jnp.bfloat16), 'tp', scatter_dimension=1,...]
    all_gather x1, waiting for transfers between devices: 17.9 us -> 0.01 us  [local(): lax.all_gather(query_weight, 'seq', axis=0, tiled=True)]
  transfers between devices with their start and end apart: 21 -> 25, of which waited for: 20 -> 20; matrix products, arithmetic and copies ran while one was open for 18% -> 19% of each run, Pallas kernels for 0% -> 0%
where the time goes in v1:
time: 1550 us; the launch traced here: 1540 us
  waiting for transfers between devices  947 us (61%)
  matrix products  224 us (14%)
  local copies, waits for them, and re-layouts  116 us (7%)
  other arithmetic  113 us (7%)
  blocking collectives  80.8 us (5%)
  starting transfers between devices  45.8 us (3%)
    ppermute x8, waiting for transfers between devices, show_the_chunk(): lax.ppermute(a_now, lane_axis, tuple(((s, s ^ answer) for s in range(n_sh...  372 us
    reduce_scatter x4, waiting for transfers between devices, feature_sum(): lax.psum_scatter(tensor.astype(jnp.bfloat16), 'tp', scatter_dimension=1,...  260 us
    psum x4, blocking collectives, row_totals(): return lax.psum((linear, squared), 'tp')  58.7 us
    reduce_scatter x1, waiting for transfers between devices, local(): lax.psum_scatter(out_grad.astype(jnp.bfloat16), 'seq', scatter_dimension=...  52.6 us
    reduce_scatter x1, waiting for transfers between devices, local(): lax.psum_scatter(value_grad.astype(jnp.bfloat16), 'seq', scatter_dimensio...  52.6 us
    reduce_scatter x1, waiting for transfers between devices, local(): lax.psum_scatter(gate_grad.astype(jnp.bfloat16), 'seq', scatter_dimension...  52.3 us
    ppermute x8, starting transfers between devices, show_the_chunk(): lax.ppermute(a_now, lane_axis, tuple(((s, s ^ answer) for s in range(n_sh...  44.8 us
    reduce_scatter x1, waiting for transfers between devices, local(): lax.psum_scatter(key_grad.astype(jnp.bfloat16), 'seq', scatter_dimension=...  42.1 us
  transfers between devices with their start and end apart: 25, of which 20 were waited for; matrix products, arithmetic and copies ran while one was open for 19% of the time, Pallas kernels for 0%

profile of v1, /device:TPU:0, one launch (start us, length us, event | category | flops | bytes accessed | tf_op | source)
XLA Modules:
  0.0 1543.4 jit_solution(11771696655694867694)
XLA Ops:
  11.1 13.7 all-reduce.4
  26.3 22.9 %collective-permute-done = bf16[1,1024,512]{2,1,0:T(8,128)(2,1)S(1)} collective-permute-done((bf16[1,1024,512]{2,1,0:T(8,128)(2,1)}, bf16[1,1024,512]{2,1,0:T(8,128)(2,1)S(1)}, u32[]{:S(2)}, u32[]{:S(2)}) %collective-permute-start) | collective-permute-done | bytes 1048608 | tf_op jit(solution)/shard_map/ppermute | solution.py:28
  54.0 88.4 %collective-permute-done.1 = bf16[2,1024,512]{2,1,0:T(8,128)(2,1)} collective-permute-done((bf16[2,1024,512]{2,1,0:T(8,128)(2,1)}, bf16[2,1024,512]{2,1,0:T(8,128)(2,1)}, u32[]{:S(2)}, u32[]{:S(2)}) %collective-permute-start.1) | collective-permute-done | bytes 2097184 | tf_op jit(solution)/shard_map/ppermute | solution.py:28
  147.8 5.2 copy.113
  153.1 7.9 reshape.520
  161.0 4.9 copy.182
  173.8 5.4 fusion.94
  183.3 9.6 convolution_convert_fusion.10
  197.5 5.1 fusion.50
  204.2 5.0 while.58
  211.4 8.8 all-gather.1
  227.9 17.3 %all-gather.22.cloned.1.call-done = bf16[16,256,512]{2,1,0:T(8,128)(2,1)} async-done(((bf16[2,256,512]{2,1,0:T(8,128)(2,1)}), bf16[16,256,512]{2,1,0:T(8,128)(2,1)}) %all-gather.22.cloned.1.call-update) | async-done | bytes 4194320 | tf_op jit(solution)/shard_map/all_gather | solution.py:40
  247.6 5.9 fusion.92
  253.5 7.4 copy.125
  267.4 16.2 %all-gather.10.cloned.1.call-done = bf16[2048,1024]{1,0:T(8,128)(2,1)} async-done(((bf16[256,1024]{1,0:T(8,128)(2,1)}), bf16[2048,1024]{1,0:T(8,128)(2,1)}) %all-gather.10.cloned.1.call-update) | async-done | bytes 4194320 | tf_op jit(solution)/shard_map/all_gather | solution.py:182
  283.5 12.0 multiply_convert_fusion.2
  295.5 27.1 %all-gather.18.cloned.1.call-done = bf16[1024,2048]{1,0:T(8,128)(2,1)} async-done(((bf16[1024,256]{1,0:T(8,128)(2,1)}), bf16[1024,2048]{1,0:T(8,128)(2,1)}) %all-gather.18.cloned.1.call-update) | async-done | bytes 4194320 | tf_op jit(solution)/shard_map/all_gather | solution.py:183
  322.6 8.3 convolution_convert_fusion.7
  333.6 62.6 %collective-permute-done.4 = bf16[1,1024,512]{2,1,0:T(8,128)(2,1)S(1)} collective-permute-done((bf16[1,1024,512]{2,1,0:T(8,128)(2,1)S(1)}, bf16[1,1024,512]{2,1,0:T(8,128)(2,1)S(1)}, u32[]{:S(2)}, u32[]{:S(2)}) %collective-permute-start.4) | collective-permute-done | bytes 1048608 | tf_op jit(solution)/shard_map/ppermute | solution.py:28
  398.9 52.6 %reduce-scatter.10.cloned.1.call-done = bf16[1024,512]{1,0:T(8,128)(2,1)} async-done(((bf16[1024,2048]{1,0:T(8,128)(2,1)}), bf16[1024,512]{1,0:T(8,128)(2,1)}) %reduce-scatter.10.cloned.1.call-update) | async-done | bytes 1048592 | tf_op jit(solution)/shard_map/reduce_scatter | solution.py:67
  453.3 21.9 %all-reduce.3 = (f32[1024]{0:T(1024)S(1)}, f32[1024]{0:T(1024)S(1)}) all-reduce(f32[1024]{0:T(1024)S(1)} %get-tuple-element.352, f32[1024]{0:T(1024)S(1)} %get-tuple-element.351), channel_id=1, replica_groups=mesh['seq'=8,'tp'=4] {'tp'}, use_global_device_ids=true, to_apply=%region_14.15 | all-reduce | flops 2048 | bytes 16384 | tf_op jit(solution)/shard_map/psum | solution.py:73
  475.8 35.5 %collective-permute-start.2 = (bf16[1,1024,512]{2,1,0:T(8,128)(2,1)S(1)}, bf16[1,1024,512]{2,1,0:T(8,128)(2,1)S(1)}, u32[]{:S(2)}, u32[]{:S(2)}) collective-permute-start(bf16[1,1024,512]{2,1,0:T(8,128)(2,1)S(1)} %get-tuple-element.424), channel_id=1, source_target_pairs={{0,1},{1,0},{2,3},{3,2},{4,5},{5,4},{6,7},{7,6},{8,9},{9,8},{10,11... | collective-permute-start | bytes 3145736 | tf_op jit(solution)/shard_map/ppermute | solution.py:28
  511.3 22.1 %collective-permute-done.2 = bf16[1,1024,512]{2,1,0:T(8,128)(2,1)S(1)} collective-permute-done((bf16[1,1024,512]{2,1,0:T(8,128)(2,1)S(1)}, bf16[1,1024,512]{2,1,0:T(8,128)(2,1)S(1)}, u32[]{:S(2)}, u32[]{:S(2)}) %collective-permute-start.2) | collective-permute-done | bytes 1048608 | tf_op jit(solution)/shard_map/ppermute | solution.py:28
  544.2 6.2 copy.135
  550.4 10.1 fusion.99
  560.5 67.6 %collective-permute-done.3 = bf16[2,1024,512]{2,1,0:T(8,128)(2,1)} collective-permute-done((bf16[2,1024,512]{2,1,0:T(8,128)(2,1)}, bf16[2,1024,512]{2,1,0:T(8,128)(2,1)}, u32[]{:S(2)}, u32[]{:S(2)}) %collective-permute-start.3) | collective-permute-done | bytes 2097184 | tf_op jit(solution)/shard_map/ppermute | solution.py:28
  632.9 6.3 copy.129
  639.2 13.8 fusion.10
  654.3 6.6 convolution_convert_fusion.5
  661.0 10.5 convolution_convert_fusion.6
  671.6 65.5 %reduce-scatter.14.cloned.1.call-done = bf16[1024,512]{1,0:T(8,128)(2,1)} async-done(((bf16[1024,2048]{1,0:T(8,128)(2,1)}), bf16[1024,512]{1,0:T(8,128)(2,1)}) %reduce-scatter.14.cloned.1.call-update) | async-done | bytes 1048592 | tf_op jit(solution)/shard_map/reduce_scatter | solution.py:67
  740.6 11.5 all-reduce.2
  752.1 64.8 %reduce-scatter.12.cloned.1.call-done = bf16[1024,512]{1,0:T(8,128)(2,1)} async-done(((bf16[1024,2048]{1,0:T(8,128)(2,1)}), bf16[1024,512]{1,0:T(8,128)(2,1)}) %reduce-scatter.12.cloned.1.call-update) | async-done | bytes 1048592 | tf_op jit(solution)/shard_map/reduce_scatter | solution.py:67
  823.5 23.2 %collective-permute-done.6 = bf16[1,1024,512]{2,1,0:T(8,128)(2,1)S(1)} collective-permute-done((bf16[1,1024,512]{2,1,0:T(8,128)(2,1)S(1)}, bf16[1,1024,512]{2,1,0:T(8,128)(2,1)S(1)}, u32[]{:S(2)}, u32[]{:S(2)}) %collective-permute-start.6) | collective-permute-done | bytes 1048608 | tf_op jit(solution)/shard_map/ppermute | solution.py:28
  856.4 85.4 %collective-permute-done.7 = bf16[2,1024,512]{2,1,0:T(8,128)(2,1)} collective-permute-done((bf16[2,1024,512]{2,1,0:T(8,128)(2,1)}, bf16[2,1024,512]{2,1,0:T(8,128)(2,1)}, u32[]{:S(2)}, u32[]{:S(2)}) %collective-permute-start.7) | collective-permute-done | bytes 2097184 | tf_op jit(solution)/shard_map/ppermute | solution.py:28
  946.7 6.3 copy.140
  953.0 14.5 fusion.80
  967.4 5.4 copy.142
  986.3 4.9 copy.145
  991.3 6.0 fusion.18
  998.9 5.4 while.59
  1007.4 8.5 convolution_convert_fusion.1
  1015.9 6.7 convolution_convert_fusion
  1039.5 6.3 convolution_convert_fusion.9
  1045.9 9.4 convolution_convert_fusion.2
  1055.4 9.4 convolution_convert_fusion.3
  1065.1 14.8 while.57
  1087.7 6.0 convolution_convert_fusion.8
  1098.6 7.5 fusion.54
  1113.7 6.3 convolution_convert_fusion.4
  1121.3 7.4 fusion.95
  1128.6 7.1 fusion.98
  1135.7 6.9 fusion.97
  1142.6 13.2 add_convert_fusion
  1155.8 18.3 %all-reduce.9.cloned.1.call-done = (bf16[2048,1024]{1,0:T(8,128)(2,1)}, bf16[1024,2048]{1,0:T(8,128)(2,1)}) async-done(((bf16[2048,1024]{1,0:T(8,128)(2,1)}, bf16[1024,2048]{1,0:T(8,128)(2,1)}), (bf16[2048,1024]{1,0:T(8,128)(2,1)}, bf16[1024,2048]{1,0:T(8,128)(2,1)})) %all-reduce.9.cloned.1.call-update) | async-done | bytes 8388624 | tf_op jit(solution)/shard_map/psum | solution.py:362
  1174.1 6.8 convert_element_type.328
  1185.3 33.2 %reduce-scatter.18.cloned.1.call-done = bf16[256,512]{1,0:T(8,128)(2,1)} async-done(((bf16[2048,512]{1,0:T(8,128)(2,1)}), bf16[256,512]{1,0:T(8,128)(2,1)}) %reduce-scatter.18.cloned.1.call-update) | async-done | bytes 262160 | tf_op jit(solution)/shard_map/reduce_scatter | solution.py:345
  1220.3 52.6 %reduce-scatter.26.cloned.1.call-done = bf16[1024,256]{1,0:T(8,128)(2,1)} async-done(((bf16[1024,2048]{1,0:T(8,128)(2,1)}), bf16[1024,256]{1,0:T(8,128)(2,1)}) %reduce-scatter.26.cloned.1.call-update) | async-done | bytes 524304 | tf_op jit(solution)/shard_map/reduce_scatter | solution.py:357
  1275.0 52.3 %reduce-scatter.24.cloned.1.call-done = bf16[256,1024]{1,0:T(8,128)(2,1)} async-done(((bf16[2048,1024]{1,0:T(8,128)(2,1)}), bf16[256,1024]{1,0:T(8,128)(2,1)}) %reduce-scatter.24.cloned.1.call-update) | async-done | bytes 524304 | tf_op jit(solution)/shard_map/reduce_scatter | solution.py:354
  1329.5 42.1 %reduce-scatter.20.cloned.1.call-done = bf16[256,512]{1,0:T(8,128)(2,1)} async-done(((bf16[2048,512]{1,0:T(8,128)(2,1)}), bf16[256,512]{1,0:T(8,128)(2,1)}) %reduce-scatter.20.cloned.1.call-update) | async-done | bytes 262160 | tf_op jit(solution)/shard_map/reduce_scatter | solution.py:348
  1373.4 52.6 %reduce-scatter.22.cloned.1.call-done = bf16[256,1024]{1,0:T(8,128)(2,1)} async-done(((bf16[2048,1024]{1,0:T(8,128)(2,1)}), bf16[256,1024]{1,0:T(8,128)(2,1)}) %reduce-scatter.22.cloned.1.call-update) | async-done | bytes 524304 | tf_op jit(solution)/shard_map/reduce_scatter | solution.py:351
  1428.1 76.8 %reduce-scatter.16.cloned.1.call-done = bf16[1024,512]{1,0:T(8,128)(2,1)} async-done(((bf16[1024,2048]{1,0:T(8,128)(2,1)}), bf16[1024,512]{1,0:T(8,128)(2,1)}) %reduce-scatter.16.cloned.1.call-update) | async-done | bytes 1048592 | tf_op jit(solution)/shard_map/reduce_scatter | solution.py:67
  1507.6 13.3 all-reduce.5
  1522.0 11.6 all-reduce.1
  (321 shorter events, 203.5 us)
Async XLA Ops:
  7.2 17.7 %copy-start.1 = (bf16[1024,512]{1,0:T(8,128)(2,1)S(1)}, bf16[1024,512]{1,0:T(8,128)(2,1)}, u32[]{:S(2)}) copy-start(bf16[1024,512]{1,0:T(8,128)(2,1)} %param.19) | copy-start | bytes 3145732
  7.2 17.7 %copy-start.66 = (f32[512]{0:T(512)S(1)}, f32[512]{0:T(512)}, u32[]{:S(2)}) copy-start(f32[512]{0:T(512)} %param.20) | copy-start | bytes 6148
  7.2 158.8 %all-gather.16.cloned.1.call-start = ((), (), s32[]{:S(2)}) async-start(), calls=%async_computation.12 | async-start | bytes 2359296 | tf_op jit(solution)/shard_map/all_gather | solution.py:180
  7.9 162.0 %all-gather.14.cloned.1.call-start = ((), (), s32[]{:S(2)}) async-start(), calls=%async_computation.11 | async-start | bytes 2359296 | tf_op jit(solution)/shard_map/all_gather | solution.py:179
  8.7 174.6 %all-gather.12.cloned.1.call-start = ((), (), s32[]{:S(2)}) async-start(), calls=%async_computation.10 | async-start | bytes 4718592 | tf_op jit(solution)/shard_map/all_gather | solution.py:181
  9.4 235.7 %all-gather.22.cloned.1.call-start = ((), (), s32[]{:S(2)}) async-start(), calls=%async_computation.24 | async-start | bytes 4718592 | tf_op jit(solution)/shard_map/all_gather | solution.py:40
  26.3 22.9 %collective-permute-start = (bf16[1,1024,512]{2,1,0:T(8,128)(2,1)}, bf16[1,1024,512]{2,1,0:T(8,128)(2,1)S(1)}, u32[]{:S(2)}, u32[]{:S(2)}) collective-permute-start(bf16[1,1024,512]{2,1,0:T(8,128)(2,1)} %get-tuple-element.437), channel_id=1, source_target_pairs={{0,1},{1,0},{2,3},{3,2},{4,5},{5,4},{6,7},{7,6},{8,9},{9,8},{10,11... | collective-permute-start | bytes 3145736 | tf_op jit(solution)/shard_map/ppermute | solution.py:28
  52.0 90.5 %collective-permute-start.1 = (bf16[2,1024,512]{2,1,0:T(8,128)(2,1)}, bf16[2,1024,512]{2,1,0:T(8,128)(2,1)}, u32[]{:S(2)}, u32[]{:S(2)}) collective-permute-start(bf16[2,1024,512]{2,1,0:T(8,128)(2,1)} %get-tuple-element.435), channel_id=1, source_target_pairs={{0,2},{1,3},{2,0},{3,1},{4,6},{5,7},{6,4},{7,5},{8,10},{9,11},{10,... | collective-permute-start | bytes 6291464 | tf_op jit(solution)/shard_map/ppermute | solution.py:28
  52.1 145.4 %copy-start.59 = (f32[512,2]{0,1:T(2,128)}, f32[512,2]{0,1:T(2,128)S(1)}, u32[]{:S(2)}) copy-start(f32[512,2]{0,1:T(2,128)S(1)} %get-tuple-element.448) | copy-start | bytes 12292
  54.0 127.6 %copy-start.39 = (f32[1024,128]{1,0:T(8,128)}, f32[1024,128]{1,0:T(8,128)S(1)}, u32[]{:S(2)}) copy-start(f32[1024,128]{1,0:T(8,128)S(1)} %get-tuple-element.440) | copy-start | bytes 1572868
  54.0 127.6 %copy-start.42 = (f32[1024,128]{1,0:T(8,128)}, f32[1024,128]{1,0:T(8,128)S(1)}, u32[]{:S(2)}) copy-start(f32[1024,128]{1,0:T(8,128)S(1)} %get-tuple-element.441) | copy-start | bytes 1572868
  173.8 5.4 copy-start.49
  173.8 5.4 copy-start.56
  183.3 38.7 %copy-start.16 = (bf16[2,512,2,256]{3,1,2,0:T(8,128)(2,1)}, bf16[2,512,2,256]{3,1,2,0:T(8,128)(2,1)S(1)}, u32[]{:S(2)}) copy-start(bf16[2,512,2,256]{3,1,2,0:T(8,128)(2,1)S(1)} %fusion.48) | copy-start | bytes 3145732
  210.2 73.3 %all-gather.10.cloned.1.call-start = ((), (), s32[]{:S(2)}) async-start(), calls=%async_computation.9 | async-start | bytes 4718592 | tf_op jit(solution)/shard_map/all_gather | solution.py:182
  210.8 111.9 %all-gather.18.cloned.1.call-start = ((), (), s32[]{:S(2)}) async-start(), calls=%async_computation.13 | async-start | bytes 4718592 | tf_op jit(solution)/shard_map/all_gather | solution.py:183
  211.3 240.2 %reduce-scatter.10.cloned.1.call-start = ((), (), s32[]{:S(2)}) async-start(), calls=%async_computation.14 | async-start | bytes 5242880 | tf_op jit(solution)/shard_map/reduce_scatter | solution.py:67
  245.4 8.0 copy-start.14
  295.5 35.4 %copy-start.57 = (bf16[1024,1024]{0,1:T(8,128)(2,1)}, bf16[1024,1024]{0,1:T(8,128)(2,1)S(1)}, u32[]{:S(2)}) copy-start(bf16[1024,1024]{0,1:T(8,128)(2,1)S(1)} %get-tuple-element.452) | copy-start | bytes 6291460
  330.9 406.2 %reduce-scatter.14.cloned.1.call-start = ((), (), s32[]{:S(2)}) async-start(), calls=%async_computation.16 | async-start | bytes 5242880 | tf_op jit(solution)/shard_map/reduce_scatter | solution.py:67
  332.1 64.1 %collective-permute-start.4 = (bf16[1,1024,512]{2,1,0:T(8,128)(2,1)S(1)}, bf16[1,1024,512]{2,1,0:T(8,128)(2,1)S(1)}, u32[]{:S(2)}, u32[]{:S(2)}) collective-permute-start(bf16[1,1024,512]{2,1,0:T(8,128)(2,1)S(1)} %bitcast.275), channel_id=1, source_target_pairs={{0,1},{1,0},{2,3},{3,2},{4,5},{5,4},{6,7},{7,6},{8,9},{9,8},{10,11... | collective-permute-start | bytes 3145736 | tf_op jit(solution)/shard_map/ppermute | solution.py:28
  398.9 76.4 %copy-start.68 = (f32[512]{0:T(512)S(1)}, f32[512]{0:T(512)}, u32[]{:S(2)}) copy-start(f32[512]{0:T(512)} %param.26) | copy-start | bytes 6148
  398.9 140.5 %collective-permute-start.5 = (bf16[2,1024,512]{2,1,0:T(8,128)(2,1)}, bf16[2,1024,512]{2,1,0:T(8,128)(2,1)}, u32[]{:S(2)}, u32[]{:S(2)}) collective-permute-start(bf16[2,1024,512]{2,1,0:T(8,128)(2,1)} %get-tuple-element.431), channel_id=1, source_target_pairs={{0,2},{1,3},{2,0},{3,1},{4,6},{5,7},{6,4},{7,5},{8,10},{9,11},{10,... | collective-permute-start | bytes 6291464 | tf_op jit(solution)/shard_map/ppermute | solution.py:28
  451.5 23.8 %copy-start.28 = (bf16[1024,512]{1,0:T(8,128)(2,1)S(1)}, bf16[1024,512]{1,0:T(8,128)(2,1)}, u32[]{:S(2)}) copy-start(bf16[1024,512]{1,0:T(8,128)(2,1)} %reduce-scatter.10.cloned.1.call-done) | copy-start | bytes 3145732
  475.8 57.6 %collective-permute-start.2 = (bf16[1,1024,512]{2,1,0:T(8,128)(2,1)S(1)}, bf16[1,1024,512]{2,1,0:T(8,128)(2,1)S(1)}, u32[]{:S(2)}, u32[]{:S(2)}) collective-permute-start(bf16[1,1024,512]{2,1,0:T(8,128)(2,1)S(1)} %get-tuple-element.424), channel_id=1, source_target_pairs={{0,1},{1,0},{2,3},{3,2},{4,5},{5,4},{6,7},{7,6},{8,9},{9,8},{10,11... | collective-permute-start | bytes 3145736 | tf_op jit(solution)/shard_map/ppermute | solution.py:28
  533.6 5.8 copy-start.37
  536.2 91.9 %collective-permute-start.3 = (bf16[2,1024,512]{2,1,0:T(8,128)(2,1)}, bf16[2,1024,512]{2,1,0:T(8,128)(2,1)}, u32[]{:S(2)}, u32[]{:S(2)}) collective-permute-start(bf16[2,1024,512]{2,1,0:T(8,128)(2,1)} %get-tuple-element.433), channel_id=1, source_target_pairs={{0,2},{1,3},{2,0},{3,1},{4,6},{5,7},{6,4},{7,5},{8,10},{9,11},{10,... | collective-permute-start | bytes 6291464 | tf_op jit(solution)/shard_map/ppermute | solution.py:28
  550.4 77.7 %copy-start.38 = (bf16[1,2,1024,512]{3,2,1,0:T(8,128)(2,1)S(1)}, bf16[1,2,1024,512]{3,2,1,0:T(8,128)(2,1)}, u32[]{:S(2)}) copy-start(bf16[1,2,1024,512]{3,2,1,0:T(8,128)(2,1)} %get-tuple-element.432) | copy-start | bytes 6291460
  639.2 15.1 copy-start.71
  660.9 156.0 %reduce-scatter.12.cloned.1.call-start = ((), (), s32[]{:S(2)}) async-start(), calls=%async_computation.15 | async-start | bytes 5242880 | tf_op jit(solution)/shard_map/reduce_scatter | solution.py:67
  671.5 393.4 %all-gather.20.cloned.1.call-start = ((), (), s32[]{:S(2)}) async-start(), calls=%async_computation.17 | async-start | bytes 4718592 | tf_op jit(solution)/shard_map/all_gather | solution.py:40
  737.1 79.8 %copy-start.51 = (bf16[1024,512]{1,0:T(8,128)(2,1)S(1)}, bf16[1024,512]{1,0:T(8,128)(2,1)}, u32[]{:S(2)}) copy-start(bf16[1024,512]{1,0:T(8,128)(2,1)} %reduce-scatter.14.cloned.1.call-done) | copy-start | bytes 3145732
  821.9 24.8 %collective-permute-start.6 = (bf16[1,1024,512]{2,1,0:T(8,128)(2,1)S(1)}, bf16[1,1024,512]{2,1,0:T(8,128)(2,1)S(1)}, u32[]{:S(2)}, u32[]{:S(2)}) collective-permute-start(bf16[1,1024,512]{2,1,0:T(8,128)(2,1)S(1)} %convert_bitcast_fusion), channel_id=1, source_target_pairs={{0,1},{1,0},{2,3},{3,2},{4,5},{5,4},{6,7},{7,6},{8,9},{9,8},{10,11... | collective-permute-start | bytes 3145736 | tf_op jit(solution)/shard_map/ppermute | solution.py:28
  848.7 93.0 %collective-permute-start.7 = (bf16[2,1024,512]{2,1,0:T(8,128)(2,1)}, bf16[2,1024,512]{2,1,0:T(8,128)(2,1)}, u32[]{:S(2)}, u32[]{:S(2)}) collective-permute-start(bf16[2,1024,512]{2,1,0:T(8,128)(2,1)} %get-tuple-element.428), channel_id=1, source_target_pairs={{0,2},{1,3},{2,0},{3,1},{4,6},{5,7},{6,4},{7,5},{8,10},{9,11},{10,... | collective-permute-start | bytes 6291464 | tf_op jit(solution)/shard_map/ppermute | solution.py:28
  972.8 4.6 copy-start.8
  972.8 5.9 copy-start.9
  991.3 6.0 copy-start.11
  1007.3 166.8 %all-reduce.9.cloned.1.call-start = ((), (), s32[]{:S(2)}) async-start(), calls=%async_computation.25 | async-start | bytes 16777216 | tf_op jit(solution)/shard_map/psum | solution.py:362
  1007.4 8.5 copy-start.48
  1007.4 8.5 copy-start.73
  1022.7 5.5 copy-start.4
  1022.7 195.8 %reduce-scatter.18.cloned.1.call-start = ((), (), s32[]{:S(2)}) async-start(), calls=%async_computation.19 | async-start | bytes 2359296 | tf_op jit(solution)/shard_map/reduce_scatter | solution.py:345
  1023.9 4.3 copy-start.6
  1023.9 4.3 copy-start.12
  1045.9 227.1 %reduce-scatter.26.cloned.1.call-start = ((), (), s32[]{:S(2)}) async-start(), calls=%async_computation.23 | async-start | bytes 4718592 | tf_op jit(solution)/shard_map/reduce_scatter | solution.py:357
  1055.4 272.0 %reduce-scatter.24.cloned.1.call-start = ((), (), s32[]{:S(2)}) async-start(), calls=%async_computation.22 | async-start | bytes 4718592 | tf_op jit(solution)/shard_map/reduce_scatter | solution.py:354
  1064.8 306.7 %reduce-scatter.20.cloned.1.call-start = ((), (), s32[]{:S(2)}) async-start(), calls=%async_computation.20 | async-start | bytes 2359296 | tf_op jit(solution)/shard_map/reduce_scatter | solution.py:348
  1065.0 14.9 copy-start.65
  1093.7 332.3 %reduce-scatter.22.cloned.1.call-start = ((), (), s32[]{:S(2)}) async-start(), calls=%async_computation.21 | async-start | bytes 4718592 | tf_op jit(solution)/shard_map/reduce_scatter | solution.py:351
  1110.0 3.7 copy-start.27
  1120.0 8.6 copy-start.53
  1120.1 384.9 %reduce-scatter.16.cloned.1.call-start = ((), (), s32[]{:S(2)}) async-start(), calls=%async_computation.18 | async-start | bytes 5242880 | tf_op jit(solution)/shard_map/reduce_scatter | solution.py:67
  1121.3 7.4 copy-start.50
  1128.6 7.1 copy-start.55
  1128.6 7.1 copy-start.72
  1135.7 6.9 copy-start.36
  1135.7 6.9 copy-start.47
  1174.1 6.8 copy-start.45
  1275.0 229.9 %copy-start.2 = (bf16[1024,512]{1,0:T(8,128)(2,1)S(1)}, bf16[1024,512]{1,0:T(8,128)(2,1)}, u32[]{:S(2)}) copy-start(bf16[1024,512]{1,0:T(8,128)(2,1)} %param.19) | copy-start | bytes 3145732
  1275.0 229.9 %copy-start.62 = (f32[1024]{0:T(1024)S(1)}, f32[1024]{0:T(1024)}, u32[]{:S(2)}) copy-start(f32[1024]{0:T(1024)} %copy-done.61) | copy-start | bytes 12292
  1275.0 229.9 %copy-start.64 = (f32[1024]{0:T(1024)S(1)}, f32[1024]{0:T(1024)}, u32[]{:S(2)}) copy-start(f32[1024]{0:T(1024)} %copy-done.63) | copy-start | bytes 12292
  1275.0 229.9 %copy-start.67 = (f32[512]{0:T(512)S(1)}, f32[512]{0:T(512)}, u32[]{:S(2)}) copy-start(f32[512]{0:T(512)} %param.20) | copy-start | bytes 6148
  1329.5 178.1 %copy-start.69 = (bf16[512]{0:T(512)(128)(2,1)S(1)}, bf16[512]{0:T(512)(128)(2,1)}, u32[]{:S(2)}) copy-start(bf16[512]{0:T(512)(128)(2,1)} %get-tuple-element.347) | copy-start | bytes 3076
  1329.5 204.2 %copy-start.21 = (f32[1024,512]{1,0:T(8,128)S(1)}, f32[1024,512]{1,0:T(8,128)}, u32[]{:S(2)}) copy-start(f32[1024,512]{1,0:T(8,128)} %copy-done.20) | copy-start | bytes 6291460
  (38 other events, 78.5 us)
Sparse Core Ops, SparseCore 0:
  9.9 30.4 all-gather.15
  42.3 27.8 all-gather.13
  72.1 36.5 all-gather.11
  210.3 34.8 all-gather.21
  246.9 36.5 all-gather.9
  285.2 37.3 all-gather.17
  331.1 120.4 reduce-scatter.9
  661.1 76.0 reduce-scatter.13
  739.4 77.4 reduce-scatter.11
  1007.4 36.6 all-gather.19
  1047.9 126.1 all-reduce.8
  1177.2 41.2 reduce-scatter.17
  1221.9 51.0 reduce-scatter.25
  1276.2 51.1 reduce-scatter.23
  1330.5 41.0 reduce-scatter.19
  1374.8 51.1 reduce-scatter.21
  1428.1 76.7 reduce-scatter.15
